TPU v7x, 256 devices: a whole 4x4x8 slice. The times are simulated.
256 devices in a mesh: fsdp: 16 (over x, z_lo, core), replica: 16 (over y, z_hi).
Axes of the slice: x: 4, y: 4, z: 8 (z_hi: 4, z_lo: 2; z = z_hi * 2 + z_lo), core: 2. Of those that a mesh axis runs over, the one named last changes fastest.
Arguments:
- weights: float32 [256, 512, 2048], P('replica', 'fsdp'), may hold values from -0.125 to 0.125
- momentum: bfloat16 [256, 512, 2048], P('replica', 'fsdp'), may hold values from -6 to 6
- tokens: bfloat16 [229376, 2048], P(('fsdp', 'replica')), may hold values from -6 to 6
- block_expert: int32 [1792], P(('fsdp', 'replica')), may hold values from 0 to 255, as said below
- owner_expert: int32 [256], replicated, may hold values from 0 to 255, as said below
Outputs:
- fresh: bfloat16 [256, 512, 2048], P(('fsdp', 'replica'))
- rollout: bfloat16 [229376, 512], P(('fsdp', 'replica'))
Inputs may be any that keep to these rules, and one draw needn't show every extreme that they name: `owner_expert`: within each group g the entries g * N to g * N + N - 1 (N the fsdp axis size) are a permutation of the expert numbers g * N to g * N + N - 1. `block_expert`: the blocks of the device at fsdp index f and replica index r are blocks (f * R + r) * 7 to (f * R + r) * 7 + 7 - 1 (R the replica axis size). Each names an expert that owner_expert assigns to fsdp index f; the 7 blocks of one device name experts of distinct groups; in every fsdp index one group is named by every device of that index.
All inputs are finite; a program needn't handle non-finite values.
Results may differ from a plain program's by a relative error of at most 0.008.
Values may be sent and summed in bfloat16 or wider, within the bound.
A program may use at most 128 MiB of HBM per device.

v0:
```python
import math
import jax
import jax.numpy as jnp
from jax import lax
from jax.sharding import PartitionSpec as P

ROWS_E = 512
COLS = 2048
ITERS = 4
quintic_one = 3.4445
quintic_two = -4.775
quintic_three = 2.0315
learn_rate = 0.05
weight_decay = 0.1
norm_eps = 1e-07


def orthogonalize(moment):
    wide = moment.astype(jnp.float32)
    state = (wide / (jnp.sqrt(jnp.sum(wide * wide)) + norm_eps)).astype(jnp.bfloat16)
    for _ in range(ITERS):
        square = lax.dot_general(
            state, state, (((1,), (1,)), ((), ())), preferred_element_type=jnp.float32
        ).astype(jnp.bfloat16)
        twice = jnp.dot(square, square, preferred_element_type=jnp.float32)
        poly = (quintic_two * square.astype(jnp.float32) + quintic_three * twice).astype(
            jnp.bfloat16
        )
        state = (
            quintic_one * state.astype(jnp.float32)
            + jnp.dot(poly, state, preferred_element_type=jnp.float32)
        ).astype(jnp.bfloat16)
    return state


def finish(master, update):
    factor = learn_rate * 0.2 * math.sqrt(max(ROWS_E, COLS))
    return (
        master * (1.0 - learn_rate * weight_decay) - factor * update.astype(jnp.float32)
    ).astype(jnp.bfloat16)


def per_device(weights, momentum, tokens, block_expert, owner_expert):
    owners = lax.axis_size("fsdp")
    groups = lax.axis_size("replica")
    group = lax.axis_index("replica")
    table = lax.dynamic_slice_in_dim(owner_expert, group * owners, owners, 0)
    local = table - group * owners
    sent_moment = jnp.take(momentum, local, axis=0)
    sent_master = jnp.take(weights, local, axis=0)
    whole_master, whole_moment = (
        lax.all_to_all(sent_master, "fsdp", split_axis=0, concat_axis=1, tiled=True),
        lax.all_to_all(
            sent_moment.astype(jnp.float32), "fsdp", split_axis=0, concat_axis=1, tiled=True
        ),
    )
    update = orthogonalize(whole_moment[0].astype(jnp.bfloat16))
    refreshed = finish(whole_master[0], update)
    fresh = refreshed[None]
    blocks = block_expert.shape[0]
    width = tokens.shape[1]
    resident = tokens.reshape(blocks, -1, width)
    target = block_expert // owners
    selector = (target[:, None] == jnp.arange(groups, dtype=jnp.int32)[None, :]).astype(
        jnp.bfloat16
    )
    outgoing = jnp.einsum(
        "bg,brd->grd", selector, resident, preferred_element_type=jnp.float32
    ).astype(jnp.bfloat16)
    product = jnp.einsum(
        "grd,od->gro",
        lax.all_to_all(outgoing, "replica", split_axis=0, concat_axis=0, tiled=True),
        refreshed,
        preferred_element_type=jnp.float32,
    ).astype(jnp.bfloat16)
    answers = lax.all_to_all(product, "replica", split_axis=0, concat_axis=0, tiled=True)
    picked = jnp.einsum(
        "bg,gro->bro", selector, answers, preferred_element_type=jnp.float32
    ).astype(jnp.bfloat16)
    rollout = picked.reshape(-1, answers.shape[2])
    return (fresh, rollout)


def solution(mesh):
    placed = (
        P("replica", "fsdp", None),
        P("replica", "fsdp", None),
        P(("fsdp", "replica"), None),
        P(("fsdp", "replica")),
        P(),
    )
    return jax.shard_map(
        per_device,
        mesh=mesh,
        in_specs=placed,
        out_specs=(P(("fsdp", "replica"), None, None), P(("fsdp", "replica"), None)),
        check_vma=False,
    )
```

profile of v0, /device:TPU:6, one launch (start us, length us, event | category | flops | bytes accessed | tf_op | source)
XLA Modules:
  0.0 393.0 jit_solution(13910733482584841381)
XLA Ops:
  0.6 0.0 copy-start
  0.7 0.9 compare_and_fusion
  1.6 0.7 copy-done
  2.2 2.0 gather_fusion.1
  4.2 3.2 select_convert_fusion
  7.4 6.1 %all-to-all-start.1 = ((bf16[16,32,2048]{2,1,0:T(8,128)(2,1)}), bf16[16,32,2048]{2,1,0:T(8,128)(2,1)S(1)}, u32[]{:S(2)}, u32[]{:S(2)}) async-start(bf16[16,32,2048]{2,1,0:T(8,128)(2,1)} %select_convert_fusion), calls=%async_computation.1 | async-start | bytes 4194304 | tf_op jit(solution)/shard_map/all_to_all | solution.py:53
  13.6 5.0 %gather_fusion = f32[16,32,2048]{2,1,0:T(8,128)} fusion(f32[16,32,2048]{2,1,0:T(8,128)} %param.5, s32[1024]{0:T(1024)S(1)} %pad_clamp_fusion), kind=kCustom, calls=%fused_computation | custom fusion | bytes 8388672 | tf_op jit(solution)/shard_map/jit(_take)/gather | solution.py:50
  18.5 4.9 %broadcast_select_fusion = f32[16,32,2048]{2,1,0:T(8,128)} fusion(f32[16,32,2048]{2,1,0:T(8,128)} %gather_fusion, pred[16]{0:T(512)(128)(4,1)S(1)} %get-tuple-element.2), kind=kLoop, calls=%fused_computation.21 | loop fusion | flops 1048576 | bytes 8388624 | tf_op jit(solution)/shard_map/jit(_take)/select_n | solution.py:50
  23.4 16.3 %all-to-all-done.1 = bf16[16,32,2048]{2,1,0:T(8,128)(2,1)S(1)} async-done(((bf16[16,32,2048]{2,1,0:T(8,128)(2,1)}), bf16[16,32,2048]{2,1,0:T(8,128)(2,1)S(1)}, u32[]{:S(2)}, u32[]{:S(2)}) %all-to-all-start.1) | async-done | bytes 2097184 | tf_op jit(solution)/shard_map/all_to_all | solution.py:53
  39.8 6.1 %all-to-all-start = ((f32[16,32,2048]{2,1,0:T(8,128)}), f32[16,32,2048]{2,1,0:T(8,128)}, u32[]{:S(2)}, u32[]{:S(2)}) async-start(f32[16,32,2048]{2,1,0:T(8,128)} %broadcast_select_fusion), calls=%async_computation | async-start | bytes 8388608 | tf_op jit(solution)/shard_map/all_to_all | solution.py:52
  45.8 8.3 %convolution_convert_fusion = bf16[16,128,2048]{2,0,1:T(8,128)(2,1)} fusion(bf16[7,128,2048]{2,1,0:T(8,128)(2,1)} %bitcast.37, s32[7]{0:T(128)S(1)} %and_select_fusion), kind=kOutput, calls=%fused_computation.4 | convolution fusion | flops 62914672 | bytes 12058652 | tf_op jit(solution)/shard_map/bg,brd->grd/dot_general | solution.py:67
  54.1 11.2 %copy.13 = bf16[16,128,2048]{2,1,0:T(8,128)(2,1)} copy(bf16[16,128,2048]{2,0,1:T(8,128)(2,1)} %convolution_convert_fusion) | data formatting | bytes 16777216 | tf_op jit(solution)/shard_map/convert_element_type | solution.py:69
  65.4 29.2 %all-to-all-done = f32[16,32,2048]{2,1,0:T(8,128)} async-done(((f32[16,32,2048]{2,1,0:T(8,128)}), f32[16,32,2048]{2,1,0:T(8,128)}, u32[]{:S(2)}, u32[]{:S(2)}) %all-to-all-start) | async-done | bytes 4194336 | tf_op jit(solution)/shard_map/all_to_all | solution.py:52
  94.6 10.4 %all-to-all-start.2 = ((bf16[16,128,2048]{2,1,0:T(8,128)(2,1)}), bf16[16,128,2048]{2,1,0:T(8,128)(2,1)}, u32[]{:S(2)}, u32[]{:S(2)}) async-start(bf16[16,128,2048]{2,1,0:T(8,128)(2,1)} %copy.13), calls=%async_computation.2 | async-start | bytes 16777216 | tf_op jit(solution)/shard_map/all_to_all | solution.py:72
  105.0 1.7 fusion.2
  107.3 0.4 fusion.3
  107.8 1.3 copy-done.2
  109.1 1.3 convolution_convert_fusion.4
  110.4 3.8 add_convert_fusion.3
  114.2 1.3 convolution_convert_fusion.3
  115.5 2.9 add_convert_fusion.2
  118.3 3.5 convolution_convert_fusion.2
  121.8 3.8 add_convert_fusion.1
  125.6 1.3 convolution_convert_fusion.1
  126.9 4.9 %broadcast_multiply_fusion = f32[16,32,2048]{2,1,0:T(8,128)} fusion(f32[16,32,2048]{2,1,0:T(8,128)} %all-to-all-done), kind=kLoop, calls=%fused_computation.20 | loop fusion | flops 1048576 | bytes 8388608 | tf_op jit(solution)/shard_map/mul | solution.py:39
  131.8 4.7 %fusion.4 = bf16[512,2048]{1,0:T(8,128)(2,1)} fusion(f32[16,32,2048]{2,1,0:T(8,128)} %broadcast_multiply_fusion, bf16[512,2048]{1,0:T(8,128)(2,1)S(1)} %add_convert_fusion.1, bf16[512,512]{1,0:T(8,128)(2,1)S(1)} %convolution_convert_fusion.1), kind=kOutput, calls=%fused_computation.10 | convolution fusion | flops 1351876608 | bytes 8912896 | tf_op jit(solution)/shard_map/dot_general | solution.py:31
  136.5 191.0 %all-to-all-done.2 = bf16[16,128,2048]{2,1,0:T(8,128)(2,1)} async-done(((bf16[16,128,2048]{2,1,0:T(8,128)(2,1)}), bf16[16,128,2048]{2,1,0:T(8,128)(2,1)}, u32[]{:S(2)}, u32[]{:S(2)}) %all-to-all-start.2) | async-done | bytes 8388640 | tf_op jit(solution)/shard_map/all_to_all | solution.py:72
  327.5 10.9 %fusion.9 = bf16[16,128,512]{2,0,1:T(8,128)(2,1)S(1)} fusion(bf16[512,2048]{1,0:T(8,128)(2,1)} %fusion.4, bf16[16,128,2048]{2,1,0:T(8,128)(2,1)} %all-to-all-done.2), kind=kOutput, calls=%fused_computation.22 | convolution fusion | flops 4296015872 | bytes 12582912 | tf_op jit(solution)/shard_map/grd,od->gro/dot_general | solution.py:70
  338.4 1.2 copy.15
  339.6 50.9 %all_to_all.28 = bf16[16,128,512]{2,1,0:T(8,128)(2,1)S(1)} all-to-all(bf16[16,128,512]{2,1,0:T(8,128)(2,1)S(1)} %copy.15), channel_id=1, replica_groups=mesh['fsdp'=16,'replica'=16] {'replica'}, dimensions={0} | all-to-all | bytes 4194304 | tf_op jit(solution)/shard_map/all_to_all | solution.py:76
  390.4 1.3 fusion.14
  391.7 1.2 copy.17
  (7 shorter events, 0.0 us)
Async XLA Ops:
  0.6 1.6 copy-start
  7.4 32.3 %all-to-all-start.1 = ((bf16[16,32,2048]{2,1,0:T(8,128)(2,1)}), bf16[16,32,2048]{2,1,0:T(8,128)(2,1)S(1)}, u32[]{:S(2)}, u32[]{:S(2)}) async-start(bf16[16,32,2048]{2,1,0:T(8,128)(2,1)} %select_convert_fusion), calls=%async_computation.1 | async-start | bytes 4194304 | tf_op jit(solution)/shard_map/all_to_all | solution.py:53
  23.4 22.4 %copy-start.3 = (s32[7]{0:T(128)S(1)}, s32[7]{0:T(128)}, u32[]{:S(2)}) copy-start(s32[7]{0:T(128)} %param.8) | copy-start | bytes 88
  39.8 54.8 %all-to-all-start = ((f32[16,32,2048]{2,1,0:T(8,128)}), f32[16,32,2048]{2,1,0:T(8,128)}, u32[]{:S(2)}, u32[]{:S(2)}) async-start(f32[16,32,2048]{2,1,0:T(8,128)} %broadcast_select_fusion), calls=%async_computation | async-start | bytes 8388608 | tf_op jit(solution)/shard_map/all_to_all | solution.py:52
  94.6 232.9 %all-to-all-start.2 = ((bf16[16,128,2048]{2,1,0:T(8,128)(2,1)}), bf16[16,128,2048]{2,1,0:T(8,128)(2,1)}, u32[]{:S(2)}, u32[]{:S(2)}) async-start(bf16[16,128,2048]{2,1,0:T(8,128)(2,1)} %copy.13), calls=%async_computation.2 | async-start | bytes 16777216 | tf_op jit(solution)/shard_map/all_to_all | solution.py:72
  107.8 1.3 copy-start.2
  339.6 53.4 %copy-start.1 = (bf16[16,32,2048]{2,1,0:T(8,128)(2,1)S(1)}, bf16[16,32,2048]{2,1,0:T(8,128)(2,1)}, u32[]{:S(2)}) copy-start(bf16[16,32,2048]{2,1,0:T(8,128)(2,1)} %param.6) | copy-start | bytes 6291460
where the time goes:
time: 394 us; the launch traced here: 393 us
  waiting for transfers between devices  237 us (60%)
  blocking collectives  50.9 us (13%)
  matrix products  42.9 us (11%)
  local copies, waits for them, and re-layouts  22.6 us (6%)
  starting transfers between devices  22.6 us (6%)
  other arithmetic  16 us (4%)
    all_to_all x1, waiting for transfers between devices, per_device(): lax.all_to_all(outgoing, 'replica', split_axis=0, concat_axis=0, tiled=True)  191 us
    all_to_all x1, blocking collectives, per_device(): lax.all_to_all(product, 'replica', split_axis=0, concat_axis=0, tiled=True)  50.9 us
    all_to_all x1, waiting for transfers between devices, per_device(): lax.all_to_all(sent_master, 'fsdp', split_axis=0, concat_axis=1, tiled=True)  29.2 us
    all_to_all x1, waiting for transfers between devices, per_device(): lax.all_to_all(sent_moment.astype(jnp.float32), 'fsdp', split_axis=0, con...  16.3 us
    dot_general x4, matrix products, orthogonalize(): jnp.dot(poly, state, preferred_element_type=jnp.float32)  15.2 us
    convert_element_type x1, local copies, waits for them, and re-layouts, per_device(): outgoing = jnp.einsum('bg,brd->grd', selector, resident, preferred_elemen...  11.2 us
    dot_general x1, matrix products, per_device(): jnp.einsum('grd,od->gro', lax.all_to_all(outgoing, 'replica', split_axis=...  10.9 us
    all_to_all x1, starting transfers between devices, per_device(): lax.all_to_all(outgoing, 'replica', split_axis=0, concat_axis=0, tiled=True)  10.4 us
  transfers between devices with their start and end apart: 3, of which 3 were waited for; matrix products, arithmetic and copies ran while one was open for 15% of the time, Pallas kernels for 0%

commit v1 on v0

--- a/solution.py
+++ b/solution.py
@@ -50,8 +50,16 @@
     sent_master = jnp.take(weights, local, axis=0)
     whole_master, whole_moment = (
         lax.all_to_all(sent_master, "fsdp", split_axis=0, concat_axis=1, tiled=True),
-        lax.all_to_all(
-            sent_moment.astype(jnp.float32), "fsdp", split_axis=0, concat_axis=1, tiled=True
+        jnp.concatenate(
+            lax.all_to_all(
+                jnp.stack(
+                    jnp.split(sent_moment.astype(jnp.float32), lax.axis_size("fsdp"), axis=0)
+                ),
+                "fsdp",
+                0,
+                0,
+            ),
+            axis=1,
         ),
     )
     update = orthogonalize(whole_moment[0].astype(jnp.bfloat16))

time: 394 us -> 403 us (1.023)
  local copies, waits for them, and re-layouts: 22.6 us -> 33.3 us
    unnamed x8 -> x23, local copies, waits for them, and re-layouts: 2.01 us -> 12 us
where the time goes in v1:
time: 403 us; the launch traced here: 402 us
  waiting for transfers between devices  237 us (59%)
  blocking collectives  50.9 us (13%)
  matrix products  42.9 us (11%)
  local copies, waits for them, and re-layouts  33.3 us (8%)
  starting transfers between devices  22.6 us (6%)
  other arithmetic  14.7 us (4%)
    all_to_all x1, waiting for transfers between devices, per_device(): lax.all_to_all(outgoing, 'replica', split_axis=0, concat_axis=0, tiled=True)  191 us
    all_to_all x1, blocking collectives, per_device(): lax.all_to_all(product, 'replica', split_axis=0, concat_axis=0, tiled=True)  50.9 us
    all_to_all x1, waiting for transfers between devices, per_device(): lax.all_to_all(sent_master, 'fsdp', split_axis=0, concat_axis=1, tiled=True)  29.2 us
    all_to_all x1, waiting for transfers between devices, per_device(): lax.all_to_all(jnp.stack(jnp.split(sent_moment.astype(jnp.float32), lax.a...  16.3 us
    dot_general x4, matrix products, orthogonalize(): jnp.dot(poly, state, preferred_element_type=jnp.float32)  15.2 us
    unnamed x23, local copies, waits for them, and re-layouts  12 us
    convert_element_type x1, local copies, waits for them, and re-layouts, per_device(): outgoing = jnp.einsum('bg,brd->grd', selector, resident, preferred_elemen...  11.2 us
    dot_general x1, matrix products, per_device(): jnp.einsum('grd,od->gro', lax.all_to_all(outgoing, 'replica', split_axis=...  10.8 us
  transfers between devices with their start and end apart: 3, of which 3 were waited for; matrix products, arithmetic and copies ran while one was open for 15% of the time, Pallas kernels for 0%

profile of v1, /device:TPU:6, one launch (start us, length us, event | category | flops | bytes accessed | tf_op | source)
XLA Modules:
  0.0 402.3 jit_solution(3207295077350428344)
XLA Ops:
  0.7 0.9 compare_and_fusion
  1.6 0.7 copy-done
  2.2 2.0 gather_fusion.1
  4.2 1.9 select_convert_fusion
  6.1 0.7 fusion.48
  7.4 0.7 fusion.46
  16.7 6.1 %all-to-all-start.1 = ((bf16[16,1,32,2048]{3,2,1,0:T(8,128)(2,1)}), bf16[16,1,32,2048]{3,2,1,0:T(8,128)(2,1)S(1)}, u32[]{:S(2)}, u32[]{:S(2)}) async-start(bf16[16,1,32,2048]{3,2,1,0:T(8,128)(2,1)} %fusion.33), calls=%async_computation.1 | async-start | bytes 4194304 | tf_op jit(solution)/shard_map/all_to_all | solution.py:54
  22.9 5.0 %gather_fusion = f32[16,32,2048]{2,1,0:T(8,128)} fusion(f32[16,32,2048]{2,1,0:T(8,128)} %param.5, s32[1024]{0:T(1024)S(1)} %pad_clamp_fusion), kind=kCustom, calls=%fused_computation | custom fusion | bytes 8388672 | tf_op jit(solution)/shard_map/jit(_take)/gather | solution.py:50
  27.9 4.9 %broadcast_select_fusion = f32[16,32,2048]{2,1,0:T(8,128)} fusion(f32[16,32,2048]{2,1,0:T(8,128)} %gather_fusion, pred[16]{0:T(512)(128)(4,1)S(1)} %get-tuple-element.2), kind=kLoop, calls=%fused_computation.21 | loop fusion | flops 1048576 | bytes 8388624 | tf_op jit(solution)/shard_map/jit(_take)/select_n | solution.py:50
  32.7 16.3 %all-to-all-done.1 = bf16[16,1,32,2048]{3,2,1,0:T(8,128)(2,1)S(1)} async-done(((bf16[16,1,32,2048]{3,2,1,0:T(8,128)(2,1)}), bf16[16,1,32,2048]{3,2,1,0:T(8,128)(2,1)S(1)}, u32[]{:S(2)}, u32[]{:S(2)}) %all-to-all-start.1) | async-done | bytes 2097184 | tf_op jit(solution)/shard_map/all_to_all | solution.py:54
  49.1 6.1 %all-to-all-start = ((f32[16,32,2048]{2,1,0:T(8,128)}), f32[16,32,2048]{2,1,0:T(8,128)}, u32[]{:S(2)}, u32[]{:S(2)}) async-start(f32[16,32,2048]{2,1,0:T(8,128)} %broadcast_select_fusion), calls=%async_computation | async-start | bytes 8388608 | tf_op jit(solution)/shard_map/all_to_all | solution.py:52
  55.1 8.3 %convolution_convert_fusion = bf16[16,128,2048]{2,0,1:T(8,128)(2,1)} fusion(bf16[7,128,2048]{2,1,0:T(8,128)(2,1)} %bitcast.101, s32[7]{0:T(128)S(1)} %and_select_fusion), kind=kOutput, calls=%fused_computation.4 | convolution fusion | flops 62914672 | bytes 12058652 | tf_op jit(solution)/shard_map/bg,brd->grd/dot_general | solution.py:75
  63.5 11.2 %copy.13 = bf16[16,128,2048]{2,1,0:T(8,128)(2,1)} copy(bf16[16,128,2048]{2,0,1:T(8,128)(2,1)} %convolution_convert_fusion) | data formatting | bytes 16777216 | tf_op jit(solution)/shard_map/convert_element_type | solution.py:77
  74.7 29.2 %all-to-all-done = f32[16,32,2048]{2,1,0:T(8,128)} async-done(((f32[16,32,2048]{2,1,0:T(8,128)}), f32[16,32,2048]{2,1,0:T(8,128)}, u32[]{:S(2)}, u32[]{:S(2)}) %all-to-all-start) | async-done | bytes 4194336 | tf_op jit(solution)/shard_map/all_to_all | solution.py:52
  103.9 10.4 %all-to-all-start.2 = ((bf16[16,128,2048]{2,1,0:T(8,128)(2,1)}), bf16[16,128,2048]{2,1,0:T(8,128)(2,1)}, u32[]{:S(2)}, u32[]{:S(2)}) async-start(bf16[16,128,2048]{2,1,0:T(8,128)(2,1)} %copy.13), calls=%async_computation.2 | async-start | bytes 16777216 | tf_op jit(solution)/shard_map/all_to_all | solution.py:80
  114.3 1.7 fusion.2
  117.1 1.3 copy-done.2
  118.4 1.3 convolution_convert_fusion.4
  119.7 3.8 add_convert_fusion.3
  123.5 1.3 convolution_convert_fusion.3
  124.8 2.9 add_convert_fusion.2
  127.7 3.5 convolution_convert_fusion.2
  131.2 3.8 add_convert_fusion.1
  135.0 1.3 convolution_convert_fusion.1
  136.2 4.9 %broadcast_multiply_fusion = f32[16,32,2048]{2,1,0:T(8,128)} fusion(f32[16,32,2048]{2,1,0:T(8,128)} %all-to-all-done), kind=kLoop, calls=%fused_computation.20 | loop fusion | flops 1048576 | bytes 8388608 | tf_op jit(solution)/shard_map/mul | solution.py:39
  141.2 4.7 %fusion.4 = bf16[512,2048]{1,0:T(8,128)(2,1)} fusion(f32[16,32,2048]{2,1,0:T(8,128)} %broadcast_multiply_fusion, bf16[512,2048]{1,0:T(8,128)(2,1)S(1)} %add_convert_fusion.1, bf16[512,512]{1,0:T(8,128)(2,1)S(1)} %convolution_convert_fusion.1), kind=kOutput, calls=%fused_computation.10 | convolution fusion | flops 1351876608 | bytes 8912896 | tf_op jit(solution)/shard_map/dot_general | solution.py:31
  145.9 191.0 %all-to-all-done.2 = bf16[16,128,2048]{2,1,0:T(8,128)(2,1)} async-done(((bf16[16,128,2048]{2,1,0:T(8,128)(2,1)}), bf16[16,128,2048]{2,1,0:T(8,128)(2,1)}, u32[]{:S(2)}, u32[]{:S(2)}) %all-to-all-start.2) | async-done | bytes 8388640 | tf_op jit(solution)/shard_map/all_to_all | solution.py:80
  336.9 10.8 %fusion.9 = bf16[16,128,512]{2,0,1:T(8,128)(2,1)S(1)} fusion(bf16[512,2048]{1,0:T(8,128)(2,1)} %fusion.4, bf16[16,128,2048]{2,1,0:T(8,128)(2,1)} %all-to-all-done.2), kind=kOutput, calls=%fused_computation.22 | convolution fusion | flops 4296015872 | bytes 12582912 | tf_op jit(solution)/shard_map/grd,od->gro/dot_general | solution.py:78
  347.7 1.2 copy.15
  348.9 50.9 %all_to_all.24 = bf16[16,128,512]{2,1,0:T(8,128)(2,1)S(1)} all-to-all(bf16[16,128,512]{2,1,0:T(8,128)(2,1)S(1)} %copy.15), channel_id=1, replica_groups=mesh['fsdp'=16,'replica'=16] {'replica'}, dimensions={0} | all-to-all | bytes 4194304 | tf_op jit(solution)/shard_map/all_to_all | solution.py:84
  399.8 1.3 fusion.14
  401.0 1.2 copy.17
  (23 shorter events, 9.7 us)
Async XLA Ops:
  0.6 1.6 copy-start
  16.7 32.3 %all-to-all-start.1 = ((bf16[16,1,32,2048]{3,2,1,0:T(8,128)(2,1)}), bf16[16,1,32,2048]{3,2,1,0:T(8,128)(2,1)S(1)}, u32[]{:S(2)}, u32[]{:S(2)}) async-start(bf16[16,1,32,2048]{3,2,1,0:T(8,128)(2,1)} %fusion.33), calls=%async_computation.1 | async-start | bytes 4194304 | tf_op jit(solution)/shard_map/all_to_all | solution.py:54
  32.7 22.4 %copy-start.3 = (s32[7]{0:T(128)S(1)}, s32[7]{0:T(128)}, u32[]{:S(2)}) copy-start(s32[7]{0:T(128)} %param.8) | copy-start | bytes 88
  49.1 54.8 %all-to-all-start = ((f32[16,32,2048]{2,1,0:T(8,128)}), f32[16,32,2048]{2,1,0:T(8,128)}, u32[]{:S(2)}, u32[]{:S(2)}) async-start(f32[16,32,2048]{2,1,0:T(8,128)} %broadcast_select_fusion), calls=%async_computation | async-start | bytes 8388608 | tf_op jit(solution)/shard_map/all_to_all | solution.py:52
  103.9 232.9 %all-to-all-start.2 = ((bf16[16,128,2048]{2,1,0:T(8,128)(2,1)}), bf16[16,128,2048]{2,1,0:T(8,128)(2,1)}, u32[]{:S(2)}, u32[]{:S(2)}) async-start(bf16[16,128,2048]{2,1,0:T(8,128)(2,1)} %copy.13), calls=%async_computation.2 | async-start | bytes 16777216 | tf_op jit(solution)/shard_map/all_to_all | solution.py:80
  117.1 1.3 copy-start.2
  348.9 53.4 %copy-start.1 = (bf16[16,32,2048]{2,1,0:T(8,128)(2,1)S(1)}, bf16[16,32,2048]{2,1,0:T(8,128)(2,1)}, u32[]{:S(2)}) copy-start(bf16[16,32,2048]{2,1,0:T(8,128)(2,1)} %param.6) | copy-start | bytes 6291460
